TPU v7x, 256 devices: a whole 4x4x8 slice. The times are simulated.
256 devices in a mesh: space: 128 (over z, x, y_hi, core), tm: 2 (over y_lo).
Axes of the slice: x: 4, y: 4 (y_hi: 2, y_lo: 2; y = y_hi * 2 + y_lo), z: 8, core: 2. Of those that a mesh axis runs over, the one named last changes fastest.
Arguments:
- features: bfloat16 [128, 2, 2, 512, 128], P('space', 'tm'), may hold values from -6 to 6
- cotangent: bfloat16 [128, 2, 2, 512, 128], P('space', 'tm'), may hold values from -6 to 6
- w_first: bfloat16 [27, 128, 128], replicated, may hold values from -0.109375 to 0.109375
- w_second: bfloat16 [27, 128, 128], replicated, may hold values from -0.109375 to 0.109375
- occupancy: int32 [128, 2, 2, 512], P('space', 'tm'), may hold values from 0 to 1, as said below
- neighbors: int32 [128, 2, 2, 27], P('space', 'tm'), may hold values from -1 to 9, as said below
- send_space: int32 [128, 2, 2, 2], P('space', 'tm'), may hold values from -1 to 1, as said below
- send_time: int32 [128, 2, 4], P('space', 'tm'), may hold values from -1 to 5, as said below
Outputs:
- grad_features: bfloat16 [128, 2, 2, 512, 128], P('space', 'tm')
- grad_first: float32 [27, 128, 128], replicated
- grad_second: float32 [27, 128, 128], replicated
Inputs may be any that keep to these rules, and one draw needn't show every extreme that they name: `occupancy`: each device has 1 to 2 active blocks, which come first; on some device all 2 are active. Blocks after the active ones have no occupied voxels. `neighbors`: entries index the extended list of 10 slots; -1 where the neighbouring block is inactive or outside the grid, and in every row of an inactive block. The relation is symmetric: a block's neighbour in one direction has it as neighbour in the opposite direction. `send_space`: positions follow the face's cells; -1 where the cell holds no active block. `send_time`: positions follow the face's cells including one block beyond each slab side, and index the own-plus-space list of 6 slots; -1 where the cell holds no active block or lies outside the grid.
All inputs are finite; a program needn't handle non-finite values.
Results may differ from a plain program's by a relative error of at most 0.0029.
Values may be sent and summed in bfloat16 or wider, within the bound.
No kernel may reach another device: no remote copies, remote signals or barrier semaphores. Data moves between devices by JAX's collectives and lax.ppermute only.
A program may use at most 128 MiB of HBM per device.

v0:
```python
import math
import jax
import jax.numpy as jnp
from jax import lax
from jax.sharding import PartitionSpec as P

EDGE = 8
offsets = [
    (first, second, third) for first in (-1, 0, 1) for second in (-1, 0, 1) for third in (-1, 0, 1)
]


def extended(value, sides, width):
    for axis, dim in sides:
        size, length = (lax.axis_size(axis), value.shape[dim])
        up = [(i, (i + 1) % size) for i in range(size - 1)]
        down = [(j, i) for i, j in up]
        last = lax.slice_in_dim(value, length - width, length, axis=dim)
        initial = lax.slice_in_dim(value, 0, width, axis=dim)
        before = lax.ppermute(last, axis, up)
        after = lax.ppermute(initial, axis, down)
        value = jnp.concatenate([before, value, after], axis=dim)
    return value


def partner(value, axis, bit):
    return lax.ppermute(value, axis, [(i, i ^ 1 << bit) for i in range(lax.axis_size(axis))])


def rim_spans(component, block_edge):
    if component < 0:
        return (slice(block_edge - 1, block_edge), slice(0, 1))
    if component == 0:
        return (slice(0, block_edge), slice(1, block_edge + 1))
    return (slice(0, 1), slice(block_edge + 1, block_edge + 2))


def assemble(store, table, block_edge):
    total_rows = store.shape[0]
    padded = jnp.concatenate([store, jnp.zeros((1,) + store.shape[1:], store.dtype)], axis=0)
    safe_rows = jnp.where(table < 0, total_rows, table)
    pieces = {}
    for number, offset in enumerate(offsets):
        source = [rim_spans(component, block_edge)[0] for component in offset]
        pieces[offset] = jnp.take(
            padded[:, source[0], source[1], source[2]], safe_rows[:, number], axis=0
        )
    layers = []
    for first in (-1, 0, 1):
        columns = []
        for second in (-1, 0, 1):
            columns.append(
                jnp.concatenate([pieces[first, second, third] for third in (-1, 0, 1)], axis=3)
            )
        layers.append(jnp.concatenate(columns, axis=2))
    return jnp.concatenate(layers, axis=1)


def window(canvas, offset, block_edge):
    starts = [1 + component for component in offset]
    region = canvas[
        :,
        starts[0] : starts[0] + block_edge,
        starts[1] : starts[1] + block_edge,
        starts[2] : starts[2] + block_edge,
    ]
    return region.reshape(-1, canvas.shape[-1])


def negate(offset):
    return tuple((-component for component in offset))


def dot_transposed(left, weight):
    return lax.dot_general(
        left, weight, (((1,), (1,)), ((), ())), preferred_element_type=jnp.float32
    )


def dot_outer(left, right):
    return lax.dot_general(
        left, right, (((0,), (0,)), ((), ())), preferred_element_type=jnp.float32
    )


def pick_rows(source, row_index, along_axis):
    size_along = source.shape[along_axis]
    zero_shape = list(source.shape)
    zero_shape[along_axis] = 1
    padded = jnp.concatenate([source, jnp.zeros(zero_shape, source.dtype)], axis=along_axis)
    return jnp.take(padded, jnp.where(row_index < 0, size_along, row_index), axis=along_axis)


def local_pass(x_tile, g_tile, mask_rows, w_first, w_second, block_edge):
    rows = mask_rows.shape[0]
    channels = w_first.shape[-1]
    pre = jnp.zeros((rows, channels), jnp.float32)
    for number, offset in enumerate(offsets):
        pre = pre + jnp.dot(
            window(x_tile, offset, block_edge), w_first[number], preferred_element_type=jnp.float32
        )
    sigmoid_pre = jax.nn.sigmoid(pre)
    hidden = (pre * sigmoid_pre * mask_rows).astype(jnp.bfloat16)
    grad_hidden = jnp.zeros((rows, channels), jnp.float32)
    second_terms = []
    for number, offset in enumerate(offsets):
        back_window = window(g_tile, negate(offset), block_edge)
        grad_hidden = grad_hidden + dot_transposed(back_window, w_second[number])
        second_terms.append(dot_outer(hidden, back_window))
    grad_pre = (grad_hidden * sigmoid_pre * (1.0 + pre * (1.0 - sigmoid_pre)) * mask_rows).astype(
        jnp.bfloat16
    )
    first_terms = [dot_outer(window(x_tile, offset, block_edge), grad_pre) for offset in offsets]
    return (grad_pre, jnp.stack(first_terms), jnp.stack(second_terms))


def body(features, cotangent, w_first, w_second, occupancy, neighbors, send_space, send_time):
    blocks, voxels, channels = (features.shape[2], features.shape[3], features.shape[4])
    block_edge = EDGE
    rim_slots = send_space.shape[3]
    mask_rows = occupancy.reshape(blocks * voxels, 1).astype(jnp.float32)
    mask_cells = occupancy.reshape(blocks, voxels, 1).astype(jnp.bfloat16)
    masked_x = features.reshape(blocks, voxels, channels) * mask_cells
    masked_g = cotangent.reshape(blocks, voxels, channels) * mask_cells
    space_sends = send_space.reshape(2, rim_slots)
    time_sends = send_time.reshape(-1)
    table = neighbors.reshape(blocks, neighbors.shape[3])
    paired = jnp.stack([masked_x, masked_g]).reshape(
        2, blocks, block_edge, block_edge, block_edge, channels
    )
    outgoing = pick_rows(paired, space_sends, 1)
    bordered = extended(outgoing, (("space", 1),), 1)
    below = bordered[:, 0]
    above = bordered[:, 3]
    base = jnp.concatenate([paired, below, above], axis=1)
    toward_time = pick_rows(base, time_sends, 1)
    across = partner(toward_time, "tm", 0)
    shaped = jnp.concatenate([base, across], axis=1)
    x_tile = assemble(shaped[0], table, block_edge)
    g_tile = assemble(shaped[1], table, block_edge)
    grad_pre, first_part, second_part = local_pass(
        x_tile, g_tile, mask_rows, w_first, w_second, block_edge
    )
    da_cells = grad_pre.reshape(blocks, block_edge, block_edge, block_edge, channels)
    da_out = pick_rows(da_cells, space_sends, 0)
    da_border = extended(da_out, (("space", 0),), 1)
    da_below = da_border[0]
    da_above = da_border[3]
    da_base = jnp.concatenate([da_cells, da_below, da_above], axis=0)
    da_toward = pick_rows(da_base, time_sends, 0)
    da_across = partner(da_toward, "tm", 0)
    da_store = jnp.concatenate([da_base, da_across], axis=0)
    da_tile = assemble(da_store, table, block_edge)
    conv_rows = jnp.zeros((blocks * voxels, channels), jnp.float32)
    for number, offset in enumerate(offsets):
        conv_rows = conv_rows + dot_transposed(
            window(da_tile, negate(offset), block_edge), w_first[number]
        )
    grad_rows = (
        cotangent.reshape(blocks * voxels, channels).astype(jnp.float32) + conv_rows * mask_rows
    )
    grad_features = grad_rows.astype(jnp.bfloat16).reshape(features.shape)
    scale = 1.0 / math.sqrt(lax.axis_size("space") * lax.axis_size("tm") * blocks * voxels)
    first_sum, second_sum = lax.psum((first_part, second_part), ("space", "tm"))
    return (grad_features, first_sum * scale, second_sum * scale)


def solution(mesh):
    placed = (
        P("space", "tm", None, None, None),
        P("space", "tm", None, None, None),
        P(),
        P(),
        P("space", "tm", None, None),
        P("space", "tm", None, None),
        P("space", "tm", None, None),
        P("space", "tm", None),
    )
    return jax.shard_map(
        body,
        mesh=mesh,
        in_specs=placed,
        out_specs=(P("space", "tm", None, None, None), P(), P()),
        check_vma=False,
    )
```

profile of v0, /device:TPU:97, one launch (start us, length us, event | category | flops | bytes accessed | tf_op | source)
XLA Modules:
  0.0 582.6 jit_solution(6243704931924489264)
XLA Ops:
  13.6 5.4 collective-permute-start
  19.0 1.9 collective-permute-start.1
  48.8 17.5 %collective-permute-done.2 = bf16[2,4,8,8,8,128]{5,4,3,2,0,1:T(8,128)(2,1)S(1)} collective-permute-done((bf16[2,4,8,8,8,128]{5,4,3,2,0,1:T(8,128)(2,1)S(1)}, bf16[2,4,8,8,8,128]{5,4,3,2,0,1:T(8,128)(2,1)S(1)}, u32[]{:S(2)}, u32[]{:S(2)}) %collective-permute-start.2) | collective-permute-done | bytes 1048608 | tf_op jit(solution)/shard_map/ppermute | solution.py:27
  67.3 2.3 slice_bitcast_fusion
  78.5 1.4 fusion.235
  79.8 1.5 fusion.239
  83.6 2.0 gather_fusion.6
  85.6 2.2 gather_fusion.41
  87.8 2.2 gather_fusion.5
  90.8 1.4 copy.318
  92.1 1.3 gather_fusion.40
  93.4 1.4 gather_fusion.4
  94.8 1.3 bitcast_select_fusion.22
  108.7 1.3 gather_fusion.57
  110.0 2.0 gather_fusion.50
  112.0 2.0 gather_fusion.14
  114.0 1.4 copy.304
  115.4 1.4 copy.314
  116.8 1.4 gather_fusion.52
  118.2 1.4 gather_fusion.16
  119.6 1.4 copy.303
  121.0 1.4 copy.313
  122.4 2.0 gather_fusion.54
  124.4 2.0 gather_fusion.18
  126.4 2.0 gather_fusion.20
  128.4 2.0 gather_fusion.56
  130.4 2.2 gather_fusion.53
  132.6 2.2 gather_fusion.17
  134.8 1.4 copy.305
  136.2 1.4 copy.315
  137.6 2.0 gather_fusion.48
  139.6 2.0 gather_fusion.12
  141.6 1.3 gather_fusion.47
  142.8 2.2 gather_fusion.11
  147.9 1.3 gather_fusion.10
  150.2 1.7 copy.294
  151.9 1.3 gather_fusion.43
  153.2 1.6 gather_fusion.7
  154.8 1.5 bitcast_select_fusion.7
  158.0 1.6 gather_fusion.45
  176.3 1.4 fusion.243
  181.2 1.4 gather_fusion.32
  185.0 1.4 gather_fusion.38
  186.5 1.6 gather_fusion.35
  188.7 1.5 fusion.244
  193.6 1.4 fusion.246
  201.7 1.4 gather_fusion.29
  203.2 1.4 gather_fusion.23
  204.7 1.6 gather_fusion.26
  277.5 7.5 %collective-permute-start.3 = (bf16[1,2,8,8,8,128]{5,4,3,2,1,0:T(8,128)(2,1)S(1)}, bf16[1,2,8,8,8,128]{5,4,3,2,1,0:T(8,128)(2,1)S(1)}, u32[]{:S(2)}, u32[]{:S(2)}) collective-permute-start(bf16[1,2,8,8,8,128]{5,4,3,2,1,0:T(8,128)(2,1)S(1)} %get-tuple-element.195), channel_id=1, source_target_pairs={{0,2},{2,4},{4,6},{6,8},{8,10},{10,12},{12,14},{14,16},{16,18},{18... | collective-permute-start | bytes 786440 | tf_op jit(solution)/shard_map/ppermute | solution.py:20
  285.0 1.9 collective-permute-start.4
  288.7 7.3 %collective-permute-done.4 = bf16[1,2,8,8,8,128]{5,4,3,2,1,0:T(8,128)(2,1)S(1)} collective-permute-done((bf16[1,2,8,8,8,128]{5,4,3,2,1,0:T(8,128)(2,1)S(1)}, bf16[1,2,8,8,8,128]{5,4,3,2,1,0:T(8,128)(2,1)S(1)}, u32[]{:S(2)}, u32[]{:S(2)}) %collective-permute-start.4) | collective-permute-done | bytes 262176 | tf_op jit(solution)/shard_map/ppermute | solution.py:21
  298.5 13.6 %collective-permute-done.5 = bf16[4,8,8,8,128]{4,3,2,1,0:T(8,128)(2,1)} collective-permute-done((bf16[4,8,8,8,128]{4,3,2,1,0:T(8,128)(2,1)}, bf16[4,8,8,8,128]{4,3,2,1,0:T(8,128)(2,1)}, u32[]{:S(2)}, u32[]{:S(2)}) %collective-permute-start.5) | collective-permute-done | bytes 524320 | tf_op jit(solution)/shard_map/ppermute | solution.py:27
  319.2 1.7 gather_fusion.59
  326.2 1.6 gather_fusion.80
  328.5 1.6 gather_fusion.65
  334.7 1.4 gather_fusion.83
  336.2 1.4 gather_fusion.77
  343.0 1.5 fusion.241
  345.6 1.6 gather_fusion.71
  348.9 1.4 gather_fusion.74
  365.0 206.1 %all-reduce.7.cloned.1.call-done = (f32[27,128,128]{2,1,0:T(8,128)}, f32[27,128,128]{2,1,0:T(8,128)}) async-done(((f32[27,128,128]{2,1,0:T(8,128)}, f32[27,128,128]{2,1,0:T(8,128)}), (f32[27,128,128]{2,1,0:T(8,128)}, f32[27,128,128]{2,1,0:T(8,128)})) %all-reduce.7.cloned.1.call-update) | async-done | bytes 3538960 | tf_op jit(solution)/shard_map/psum | solution.py:164
  571.1 3.0 broadcast_multiply_fusion
  574.1 1.4 broadcast_multiply_fusion.1
  (693 shorter events, 212.3 us)
Async XLA Ops:
  7.2 563.9 %all-reduce.7.cloned.1.call-start = ((), (), s32[]{:S(2)}) async-start(), calls=%async_computation | async-start | bytes 7077888 | tf_op jit(solution)/shard_map/psum | solution.py:164
  8.6 4.7 copy-start.120
  13.5 7.4 %copy-start.125 = (s32[1,1,4]{2,1,0:T(1,128)S(1)}, s32[1,1,4]{2,1,0:T(1,128)}, u32[]{:S(2)}) copy-start(s32[1,1,4]{2,1,0:T(1,128)} %param.31) | copy-start | bytes 52
  13.6 28.7 %collective-permute-start = (bf16[2,1,2,8,8,8,128]{6,5,4,3,2,0,1:T(8,128)(2,1)S(1)}, bf16[2,1,2,8,8,8,128]{6,5,4,3,2,0,1:T(8,128)(2,1)S(1)}, u32[]{:S(2)}, u32[]{:S(2)}) collective-permute-start(bf16[2,1,2,8,8,8,128]{6,5,4,3,2,0,1:T(8,128)(2,1)S(1)} %get-tuple-element.121), channel_id=1, source_target_pairs={{0,2},{2,4},{4,6},{6,8},{8,10},{10,12},{12,14},{14,16},{16,18},{18... | collective-permute-start | bytes 1572872 | tf_op jit(solution)/shard_map/ppermute | solution.py:20
  19.0 23.3 %collective-permute-start.1 = (bf16[2,1,2,8,8,8,128]{6,5,4,3,2,0,1:T(8,128)(2,1)S(1)}, bf16[2,1,2,8,8,8,128]{6,5,4,3,2,0,1:T(8,128)(2,1)S(1)}, u32[]{:S(2)}, u32[]{:S(2)}) collective-permute-start(bf16[2,1,2,8,8,8,128]{6,5,4,3,2,0,1:T(8,128)(2,1)S(1)} %get-tuple-element.120), channel_id=1, source_target_pairs={{2,0},{4,2},{6,4},{8,6},{10,8},{12,10},{14,12},{16,14},{18,16},{20... | collective-permute-start | bytes 1572872 | tf_op jit(solution)/shard_map/ppermute | solution.py:21
  20.9 23.3 %copy-start.122 = (pred[4]{0:T(512)(128)(4,1)}, pred[4]{0:T(512)(128)(4,1)S(1)}, u32[]{:S(2)}) copy-start(pred[4]{0:T(512)(128)(4,1)S(1)} %compare_and_fusion.27) | copy-start | bytes 16
  28.0 15.4 %copy-start.104 = (s32[1024]{0:T(1024)}, s32[1024]{0:T(1024)S(1)}, u32[]{:S(2)}) copy-start(s32[1024]{0:T(1024)S(1)} %pad_clamp_fusion.27) | copy-start | bytes 12292
  44.2 2.9 copy-start.38
  44.2 3.7 copy-start.40
  44.4 21.8 %collective-permute-start.2 = (bf16[2,4,8,8,8,128]{5,4,3,2,0,1:T(8,128)(2,1)S(1)}, bf16[2,4,8,8,8,128]{5,4,3,2,0,1:T(8,128)(2,1)S(1)}, u32[]{:S(2)}, u32[]{:S(2)}) collective-permute-start(bf16[2,4,8,8,8,128]{5,4,3,2,0,1:T(8,128)(2,1)S(1)} %select_bitcast_fusion), channel_id=1, source_target_pairs={{0,1},{1,0},{2,3},{3,2},{4,5},{5,4},{6,7},{7,6},{8,9},{9,8},{10,11... | collective-permute-start | bytes 3145736 | tf_op jit(solution)/shard_map/ppermute | solution.py:27
  150.2 11.6 %copy-start.86 = (bf16[2,8,128]{2,1,0:T(8,128)(2,1)S(1)}, bf16[2,8,128]{2,1,0:T(8,128)(2,1)}, u32[]{:S(2)}) copy-start(bf16[2,8,128]{2,1,0:T(8,128)(2,1)} %gather_fusion.42) | copy-start | bytes 12292
  150.2 11.6 %copy-start.87 = (bf16[2,8,128]{2,1,0:T(8,128)(2,1)S(1)}, bf16[2,8,128]{2,1,0:T(8,128)(2,1)}, u32[]{:S(2)}) copy-start(bf16[2,8,128]{2,1,0:T(8,128)(2,1)} %gather_fusion.6) | copy-start | bytes 12292
  154.8 14.7 %copy-start.66 = (bf16[2,8,8,128]{3,2,1,0:T(8,128)(2,1)S(1)}, bf16[2,8,8,128]{3,2,1,0:T(8,128)(2,1)}, u32[]{:S(2)}) copy-start(bf16[2,8,8,128]{3,2,1,0:T(8,128)(2,1)} %gather_fusion.53) | copy-start | bytes 98308
  154.8 14.7 %copy-start.67 = (bf16[2,8,8,128]{3,2,1,0:T(8,128)(2,1)S(1)}, bf16[2,8,8,128]{3,2,1,0:T(8,128)(2,1)}, u32[]{:S(2)}) copy-start(bf16[2,8,8,128]{3,2,1,0:T(8,128)(2,1)} %gather_fusion.17) | copy-start | bytes 98308
  156.2 14.7 %copy-start.68 = (bf16[2,8,8,128]{3,2,1,0:T(8,128)(2,1)S(1)}, bf16[2,8,8,128]{3,2,1,0:T(8,128)(2,1)}, u32[]{:S(2)}) copy-start(bf16[2,8,8,128]{3,2,1,0:T(8,128)(2,1)} %gather_fusion.47) | copy-start | bytes 98308
  156.3 14.7 %copy-start.69 = (bf16[2,8,8,128]{3,2,1,0:T(8,128)(2,1)S(1)}, bf16[2,8,8,128]{3,2,1,0:T(8,128)(2,1)}, u32[]{:S(2)}) copy-start(bf16[2,8,8,128]{3,2,1,0:T(8,128)(2,1)} %gather_fusion.11) | copy-start | bytes 98308
  177.7 3.4 copy-start.98
  177.8 4.9 copy-start.91
  177.8 5.6 copy-start.100
  177.8 6.4 %copy-start.102 = (pred[2]{0:T(512)(128)(4,1)S(1)}, pred[2]{0:T(512)(128)(4,1)}, u32[]{:S(2)}) copy-start(pred[2]{0:T(512)(128)(4,1)} %get-tuple-element.270) | copy-start | bytes 10
  177.8 7.1 %copy-start.95 = (pred[2]{0:T(512)(128)(4,1)S(1)}, pred[2]{0:T(512)(128)(4,1)}, u32[]{:S(2)}) copy-start(pred[2]{0:T(512)(128)(4,1)} %get-tuple-element.271) | copy-start | bytes 10
  177.8 8.6 %copy-start.93 = (pred[2]{0:T(512)(128)(4,1)S(1)}, pred[2]{0:T(512)(128)(4,1)}, u32[]{:S(2)}) copy-start(pred[2]{0:T(512)(128)(4,1)} %get-tuple-element.269) | copy-start | bytes 10
  177.8 10.3 %copy-start.90 = (pred[2]{0:T(512)(128)(4,1)S(1)}, pred[2]{0:T(512)(128)(4,1)}, u32[]{:S(2)}) copy-start(pred[2]{0:T(512)(128)(4,1)} %get-tuple-element.272) | copy-start | bytes 10
  195.1 2.8 copy-start.79
  195.1 3.6 copy-start.78
  195.1 4.3 copy-start.77
  277.3 10.5 %copy-start.44 = (bf16[2,8,8,8,128]{4,3,2,1,0:T(8,128)(2,1)S(1)}, bf16[2,8,8,8,128]{4,3,2,1,0:T(8,128)(2,1)}, u32[]{:S(2)}) copy-start(bf16[2,8,8,8,128]{4,3,2,1,0:T(8,128)(2,1)} %get-tuple-element.140) | copy-start | bytes 786436
  277.5 11.3 %collective-permute-start.3 = (bf16[1,2,8,8,8,128]{5,4,3,2,1,0:T(8,128)(2,1)S(1)}, bf16[1,2,8,8,8,128]{5,4,3,2,1,0:T(8,128)(2,1)S(1)}, u32[]{:S(2)}, u32[]{:S(2)}) collective-permute-start(bf16[1,2,8,8,8,128]{5,4,3,2,1,0:T(8,128)(2,1)S(1)} %get-tuple-element.195), channel_id=1, source_target_pairs={{0,2},{2,4},{4,6},{6,8},{8,10},{10,12},{12,14},{14,16},{16,18},{18... | collective-permute-start | bytes 786440 | tf_op jit(solution)/shard_map/ppermute | solution.py:20
  285.0 11.1 %collective-permute-start.4 = (bf16[1,2,8,8,8,128]{5,4,3,2,1,0:T(8,128)(2,1)S(1)}, bf16[1,2,8,8,8,128]{5,4,3,2,1,0:T(8,128)(2,1)S(1)}, u32[]{:S(2)}, u32[]{:S(2)}) collective-permute-start(bf16[1,2,8,8,8,128]{5,4,3,2,1,0:T(8,128)(2,1)S(1)} %get-tuple-element.194), channel_id=1, source_target_pairs={{2,0},{4,2},{6,4},{8,6},{10,8},{12,10},{14,12},{16,14},{18,16},{20... | collective-permute-start | bytes 786440 | tf_op jit(solution)/shard_map/ppermute | solution.py:21
  297.9 14.2 %collective-permute-start.5 = (bf16[4,8,8,8,128]{4,3,2,1,0:T(8,128)(2,1)}, bf16[4,8,8,8,128]{4,3,2,1,0:T(8,128)(2,1)}, u32[]{:S(2)}, u32[]{:S(2)}) collective-permute-start(bf16[4,8,8,8,128]{4,3,2,1,0:T(8,128)(2,1)} %broadcast_select_fusion), channel_id=1, source_target_pairs={{0,1},{1,0},{2,3},{3,2},{4,5},{5,4},{6,7},{7,6},{8,9},{9,8},{10,11... | collective-permute-start | bytes 1572872 | tf_op jit(solution)/shard_map/ppermute | solution.py:27
  314.9 6.0 %copy-start.106 = (pred[2]{0:T(512)(128)(4,1)S(1)}, pred[2]{0:T(512)(128)(4,1)}, u32[]{:S(2)}) copy-start(pred[2]{0:T(512)(128)(4,1)} %get-tuple-element.303) | copy-start | bytes 10
  314.9 6.8 %copy-start.112 = (pred[2]{0:T(512)(128)(4,1)S(1)}, pred[2]{0:T(512)(128)(4,1)}, u32[]{:S(2)}) copy-start(pred[2]{0:T(512)(128)(4,1)} %get-tuple-element.302) | copy-start | bytes 10
  314.9 7.6 %copy-start.113 = (pred[2]{0:T(512)(128)(4,1)S(1)}, pred[2]{0:T(512)(128)(4,1)}, u32[]{:S(2)}) copy-start(pred[2]{0:T(512)(128)(4,1)} %get-tuple-element.296) | copy-start | bytes 10
  319.1 11.7 %copy-start.64 = (bf16[11,1,8,1,128]{4,3,2,1,0:T(2,128)(2,1)S(1)}, bf16[11,1,8,1,128]{4,3,2,1,0:T(2,128)(2,1)}, u32[]{:S(2)}) copy-start(bf16[11,1,8,1,128]{4,3,2,1,0:T(2,128)(2,1)} %get-tuple-element.54) | copy-start | bytes 67588
  319.1 13.2 %copy-start.63 = (bf16[11,1,8,1,128]{4,3,2,1,0:T(2,128)(2,1)S(1)}, bf16[11,1,8,1,128]{4,3,2,1,0:T(2,128)(2,1)}, u32[]{:S(2)}) copy-start(bf16[11,1,8,1,128]{4,3,2,1,0:T(2,128)(2,1)} %get-tuple-element.55) | copy-start | bytes 67588
  319.1 13.9 %copy-start.96 = (pred[2]{0:T(512)(128)(4,1)S(1)}, pred[2]{0:T(512)(128)(4,1)}, u32[]{:S(2)}) copy-start(pred[2]{0:T(512)(128)(4,1)} %get-tuple-element.271) | copy-start | bytes 10
  319.1 14.0 %copy-start.62 = (bf16[11,8,1,1,128]{4,3,2,1,0:T(2,128)(2,1)S(1)}, bf16[11,8,1,1,128]{4,3,2,1,0:T(2,128)(2,1)}, u32[]{:S(2)}) copy-start(bf16[11,8,1,1,128]{4,3,2,1,0:T(2,128)(2,1)} %get-tuple-element.61) | copy-start | bytes 67588
  319.1 14.7 %copy-start.124 = (pred[2]{0:T(512)(128)(4,1)S(1)}, pred[2]{0:T(512)(128)(4,1)}, u32[]{:S(2)}) copy-start(pred[2]{0:T(512)(128)(4,1)} %compare_and_fusion.19) | copy-start | bytes 10
  319.2 14.7 %copy-start.61 = (bf16[11,8,1,1,128]{4,3,2,1,0:T(2,128)(2,1)S(1)}, bf16[11,8,1,1,128]{4,3,2,1,0:T(2,128)(2,1)}, u32[]{:S(2)}) copy-start(bf16[11,8,1,1,128]{4,3,2,1,0:T(2,128)(2,1)} %get-tuple-element.62) | copy-start | bytes 67588
  319.2 15.4 %copy-start.111 = (pred[2]{0:T(512)(128)(4,1)S(1)}, pred[2]{0:T(512)(128)(4,1)}, u32[]{:S(2)}) copy-start(pred[2]{0:T(512)(128)(4,1)} %get-tuple-element.298) | copy-start | bytes 10
  320.8 15.3 %copy-start.94 = (pred[2]{0:T(512)(128)(4,1)S(1)}, pred[2]{0:T(512)(128)(4,1)}, u32[]{:S(2)}) copy-start(pred[2]{0:T(512)(128)(4,1)} %get-tuple-element.269) | copy-start | bytes 10
  320.8 16.8 %copy-start.92 = (pred[2]{0:T(512)(128)(4,1)S(1)}, pred[2]{0:T(512)(128)(4,1)}, u32[]{:S(2)}) copy-start(pred[2]{0:T(512)(128)(4,1)} %get-tuple-element.275) | copy-start | bytes 10
  320.9 16.8 %copy-start.76 = (bf16[11,1,1,1,128]{4,3,2,1,0:T(2,128)(2,1)S(1)}, bf16[11,1,1,1,128]{4,3,2,1,0:T(2,128)(2,1)}, u32[]{:S(2)}) copy-start(bf16[11,1,1,1,128]{4,3,2,1,0:T(2,128)(2,1)} %get-tuple-element.43) | copy-start | bytes 8452
  320.9 17.5 %copy-start.101 = (pred[2]{0:T(512)(128)(4,1)S(1)}, pred[2]{0:T(512)(128)(4,1)}, u32[]{:S(2)}) copy-start(pred[2]{0:T(512)(128)(4,1)} %get-tuple-element.268) | copy-start | bytes 10
  321.0 17.5 %copy-start.75 = (bf16[11,1,1,1,128]{4,3,2,1,0:T(2,128)(2,1)S(1)}, bf16[11,1,1,1,128]{4,3,2,1,0:T(2,128)(2,1)}, u32[]{:S(2)}) copy-start(bf16[11,1,1,1,128]{4,3,2,1,0:T(2,128)(2,1)} %get-tuple-element.44) | copy-start | bytes 8452
  321.0 18.2 %copy-start.103 = (pred[2]{0:T(512)(128)(4,1)S(1)}, pred[2]{0:T(512)(128)(4,1)}, u32[]{:S(2)}) copy-start(pred[2]{0:T(512)(128)(4,1)} %get-tuple-element.270) | copy-start | bytes 10
  321.0 18.3 %copy-start.74 = (bf16[11,1,1,1,128]{4,3,2,1,0:T(2,128)(2,1)S(1)}, bf16[11,1,1,1,128]{4,3,2,1,0:T(2,128)(2,1)}, u32[]{:S(2)}) copy-start(bf16[11,1,1,1,128]{4,3,2,1,0:T(2,128)(2,1)} %get-tuple-element.45) | copy-start | bytes 8452
  321.0 19.0 %copy-start.99 = (pred[2]{0:T(512)(128)(4,1)S(1)}, pred[2]{0:T(512)(128)(4,1)}, u32[]{:S(2)}) copy-start(pred[2]{0:T(512)(128)(4,1)} %get-tuple-element.274) | copy-start | bytes 10
  321.0 19.0 %copy-start.73 = (bf16[11,1,1,1,128]{4,3,2,1,0:T(2,128)(2,1)S(1)}, bf16[11,1,1,1,128]{4,3,2,1,0:T(2,128)(2,1)}, u32[]{:S(2)}) copy-start(bf16[11,1,1,1,128]{4,3,2,1,0:T(2,128)(2,1)} %get-tuple-element.42) | copy-start | bytes 8452
  321.0 19.7 %copy-start.119 = (pred[2]{0:T(512)(128)(4,1)S(1)}, pred[2]{0:T(512)(128)(4,1)}, u32[]{:S(2)}) copy-start(pred[2]{0:T(512)(128)(4,1)} %get-tuple-element.276) | copy-start | bytes 10
  344.5 2.7 copy-start.105
  344.5 2.8 copy-start.60
  344.5 3.5 copy-start.110
  344.5 4.3 copy-start.108
  344.5 5.8 copy-start.109
  344.5 6.5 %copy-start.107 = (pred[2]{0:T(512)(128)(4,1)S(1)}, pred[2]{0:T(512)(128)(4,1)}, u32[]{:S(2)}) copy-start(pred[2]{0:T(512)(128)(4,1)} %get-tuple-element.284) | copy-start | bytes 10
  344.5 6.6 %copy-start.72 = (bf16[11,1,1,1,128]{4,3,2,1,0:T(2,128)(2,1)S(1)}, bf16[11,1,1,1,128]{4,3,2,1,0:T(2,128)(2,1)}, u32[]{:S(2)}) copy-start(bf16[11,1,1,1,128]{4,3,2,1,0:T(2,128)(2,1)} %get-tuple-element.47) | copy-start | bytes 8452
  344.5 7.3 %copy-start.117 = (pred[2]{0:T(512)(128)(4,1)S(1)}, pred[2]{0:T(512)(128)(4,1)}, u32[]{:S(2)}) copy-start(pred[2]{0:T(512)(128)(4,1)} %get-tuple-element.279) | copy-start | bytes 10
  344.5 7.4 %copy-start.71 = (bf16[11,1,1,1,128]{4,3,2,1,0:T(2,128)(2,1)S(1)}, bf16[11,1,1,1,128]{4,3,2,1,0:T(2,128)(2,1)}, u32[]{:S(2)}) copy-start(bf16[11,1,1,1,128]{4,3,2,1,0:T(2,128)(2,1)} %get-tuple-element.48) | copy-start | bytes 8452
  344.5 8.0 %copy-start.116 = (pred[2]{0:T(512)(128)(4,1)S(1)}, pred[2]{0:T(512)(128)(4,1)}, u32[]{:S(2)}) copy-start(pred[2]{0:T(512)(128)(4,1)} %get-tuple-element.283) | copy-start | bytes 10
  344.6 8.1 %copy-start.70 = (bf16[11,1,1,1,128]{4,3,2,1,0:T(2,128)(2,1)S(1)}, bf16[11,1,1,1,128]{4,3,2,1,0:T(2,128)(2,1)}, u32[]{:S(2)}) copy-start(bf16[11,1,1,1,128]{4,3,2,1,0:T(2,128)(2,1)} %get-tuple-element.49) | copy-start | bytes 8452
  344.6 8.8 %copy-start.114 = (pred[2]{0:T(512)(128)(4,1)S(1)}, pred[2]{0:T(512)(128)(4,1)}, u32[]{:S(2)}) copy-start(pred[2]{0:T(512)(128)(4,1)} %get-tuple-element.285) | copy-start | bytes 10
  344.6 9.6 %copy-start.115 = (pred[2]{0:T(512)(128)(4,1)S(1)}, pred[2]{0:T(512)(128)(4,1)}, u32[]{:S(2)}) copy-start(pred[2]{0:T(512)(128)(4,1)} %get-tuple-element.277) | copy-start | bytes 10
  571.1 3.0 copy-start.42
  (69 other events, 100.0 us)
Sparse Core Ops, SparseCore 0:
  298.5 272.5 all-reduce.6
where the time goes:
time: 591 us; the launch traced here: 583 us
  waiting for transfers between devices  245 us (41%)
  local copies, waits for them, and re-layouts  168 us (28%)
  matrix products  71.6 us (12%)
  other arithmetic  63.2 us (11%)
  starting transfers between devices  18.1 us (3%)
  between operations  17.1 us (3%)
    psum x1, waiting for transfers between devices, body(): first_sum, second_sum = lax.psum((first_part, second_part), ('space', 'tm'))  206 us
    gather x81, local copies, waits for them, and re-layouts, assemble(): jnp.take(padded[:, source[0], source[1], source[2]], safe_rows[:, number]...  97.2 us
    dot_general x54, matrix products, dot_transposed(): lax.dot_general(left, weight, (((1,), (1,)), ((), ())), preferred_element...  34.2 us
    unnamed x313, local copies, waits for them, and re-layouts  33.7 us
    dot_general x54, matrix products, dot_outer(): lax.dot_general(left, right, (((0,), (0,)), ((), ())), preferred_element_...  31.7 us
    ppermute x2, waiting for transfers between devices, partner(): lax.ppermute(value, axis, [(i, i ^ 1 << bit) for i in range(lax.axis_size...  31.1 us
    select_n x81, other arithmetic, assemble(): jnp.take(padded[:, source[0], source[1], source[2]], safe_rows[:, number]...  22.3 us
    gather x23, other arithmetic  13.7 us
  transfers between devices with their start and end apart: 7, of which 4 were waited for; matrix products, arithmetic and copies ran while one was open for 13% of the time, Pallas kernels for 0%

commit v1 on v0

--- a/solution.py
+++ b/solution.py
@@ -8,6 +8,11 @@
 offsets = [
     (first, second, third) for first in (-1, 0, 1) for second in (-1, 0, 1) for third in (-1, 0, 1)
 ]
+
+
+def groups_build(vec):
+    reply = lax.psum(lax.psum(vec, "tm"), "space")
+    return reply
 
 
 def extended(value, sides, width):
@@ -161,7 +166,7 @@
     )
     grad_features = grad_rows.astype(jnp.bfloat16).reshape(features.shape)
     scale = 1.0 / math.sqrt(lax.axis_size("space") * lax.axis_size("tm") * blocks * voxels)
-    first_sum, second_sum = lax.psum((first_part, second_part), ("space", "tm"))
+    first_sum, second_sum = groups_build((first_part, second_part))
     return (grad_features, first_sum * scale, second_sum * scale)
 
 

time: 591 us -> 1690 us (2.86)
  the two profiles are of different devices: /device:TPU:97 before, /device:TPU:1 now
where the time goes in v1:
time: 1690 us
  waiting for transfers between devices  1350 us (80%)
  local copies, waits for them, and re-layouts  169 us (10%)
  matrix products  71.6 us (4%)
  other arithmetic  63.4 us (4%)
  starting transfers between devices  17.7 us (1%)
  between operations  17.2 us (1%)
    psum x2, waiting for transfers between devices, groups_build(): reply = lax.psum(lax.psum(vec, 'tm'), 'space')  1310 us
    gather x81, local copies, waits for them, and re-layouts, assemble(): jnp.take(padded[:, source[0], source[1], source[2]], safe_rows[:, number]...  99.4 us
    dot_general x54, matrix products, dot_transposed(): lax.dot_general(left, weight, (((1,), (1,)), ((), ())), preferred_element...  34.2 us
  transfers between devices with their start and end apart: 8, of which 5 were waited for; matrix products, arithmetic and copies ran while one was open for 5% of the time, Pallas kernels for 0%

profile of v1, /device:TPU:1, one launch (start us, length us, event | category | flops | bytes accessed | tf_op | source)
XLA Modules:
  0.0 1685.7 jit_solution(15585695239779384675)
XLA Ops:
  13.6 6.2 collective-permute-start
  19.8 1.9 collective-permute-start.1
  49.8 19.2 %collective-permute-done.2 = bf16[2,4,8,8,8,128]{5,4,3,2,0,1:T(8,128)(2,1)S(1)} collective-permute-done((bf16[2,4,8,8,8,128]{5,4,3,2,0,1:T(8,128)(2,1)S(1)}, bf16[2,4,8,8,8,128]{5,4,3,2,0,1:T(8,128)(2,1)S(1)}, u32[]{:S(2)}, u32[]{:S(2)}) %collective-permute-start.2) | collective-permute-done | bytes 1048608 | tf_op jit(solution)/shard_map/ppermute | solution.py:32
  70.0 2.3 slice_bitcast_fusion
  81.1 1.4 fusion.235
  82.5 1.5 fusion.239
  86.2 2.0 gather_fusion.6
  88.2 2.2 gather_fusion.41
  90.4 2.2 gather_fusion.5
  93.4 1.4 copy.318
  94.8 1.3 gather_fusion.40
  96.1 1.4 gather_fusion.4
  97.5 1.4 bitcast_select_fusion.22
  112.7 2.0 gather_fusion.50
  114.6 2.0 gather_fusion.14
  116.6 1.4 copy.304
  118.0 1.4 copy.314
  119.4 1.4 gather_fusion.52
  120.8 1.4 gather_fusion.16
  122.3 1.4 copy.303
  123.6 1.4 copy.313
  125.0 2.0 gather_fusion.54
  127.0 2.0 gather_fusion.18
  129.0 2.0 gather_fusion.20
  131.0 2.0 gather_fusion.56
  133.0 2.2 gather_fusion.53
  135.2 2.2 gather_fusion.17
  137.4 1.4 copy.305
  138.8 1.4 copy.315
  140.2 2.0 gather_fusion.48
  142.2 2.0 gather_fusion.12
  144.2 1.3 gather_fusion.47
  145.5 2.2 gather_fusion.11
  150.5 1.3 gather_fusion.10
  152.8 1.7 copy.294
  154.5 1.3 gather_fusion.43
  155.8 1.6 gather_fusion.7
  157.4 1.5 bitcast_select_fusion.7
  160.7 1.6 gather_fusion.45
  178.8 1.4 fusion.243
  183.7 1.4 gather_fusion.32
  187.5 1.4 gather_fusion.38
  189.0 1.6 gather_fusion.35
  191.1 1.6 fusion.244
  196.1 1.4 fusion.246
  204.2 1.4 gather_fusion.29
  205.7 1.4 gather_fusion.23
  207.2 1.6 gather_fusion.26
  279.9 5.8 collective-permute-start.3
  285.7 1.9 collective-permute-start.4
  289.4 5.5 collective-permute-done.4
  297.8 9.2 collective-permute-done.5
  314.1 1.8 gather_fusion.59
  319.6 1.6 gather_fusion.80
  321.9 1.6 gather_fusion.65
  327.9 1.4 gather_fusion.83
  330.0 1.4 gather_fusion.77
  339.5 1.6 gather_fusion.71
  342.8 1.4 gather_fusion.74
  344.3 1.4 gather_fusion.68
  355.8 53.2 %all-reduce.11.cloned.1.call-done = (f32[27,128,128]{2,1,0:T(8,128)}, f32[27,128,128]{2,1,0:T(8,128)}) async-done(((f32[27,128,128]{2,1,0:T(8,128)}, f32[27,128,128]{2,1,0:T(8,128)}), (f32[27,128,128]{2,1,0:T(8,128)}, f32[27,128,128]{2,1,0:T(8,128)})) %all-reduce.11.cloned.1.call-update) | async-done | bytes 3538960 | tf_op jit(solution)/shard_map/psum | solution.py:14
  414.8 1259.4 %all-reduce.9.cloned.1.call-done = (f32[27,128,128]{2,1,0:T(8,128)}, f32[27,128,128]{2,1,0:T(8,128)}) async-done(((f32[27,128,128]{2,1,0:T(8,128)}, f32[27,128,128]{2,1,0:T(8,128)}), (f32[27,128,128]{2,1,0:T(8,128)}, f32[27,128,128]{2,1,0:T(8,128)})) %all-reduce.9.cloned.1.call-update) | async-done | bytes 3538960 | tf_op jit(solution)/shard_map/psum | solution.py:14
  1674.2 3.0 broadcast_multiply_fusion
  1677.2 1.4 broadcast_multiply_fusion.1
  (714 shorter events, 215.4 us)
Async XLA Ops:
  7.2 401.8 %all-reduce.11.cloned.1.call-start = ((), (), s32[]{:S(2)}) async-start(), calls=%async_computation.1 | async-start | bytes 7077888 | tf_op jit(solution)/shard_map/psum | solution.py:14
  8.6 4.7 copy-start.127
  13.5 8.2 copy-start.134
  13.6 29.6 %collective-permute-start = (bf16[2,1,2,8,8,8,128]{6,5,4,3,2,0,1:T(8,128)(2,1)S(1)}, bf16[2,1,2,8,8,8,128]{6,5,4,3,2,0,1:T(8,128)(2,1)S(1)}, u32[]{:S(2)}, u32[]{:S(2)}) collective-permute-start(bf16[2,1,2,8,8,8,128]{6,5,4,3,2,0,1:T(8,128)(2,1)S(1)} %get-tuple-element.123), channel_id=1, source_target_pairs={{0,2},{2,4},{4,6},{6,8},{8,10},{10,12},{12,14},{14,16},{16,18},{18... | collective-permute-start | bytes 1572872 | tf_op jit(solution)/shard_map/ppermute | solution.py:25
  19.8 23.4 %collective-permute-start.1 = (bf16[2,1,2,8,8,8,128]{6,5,4,3,2,0,1:T(8,128)(2,1)S(1)}, bf16[2,1,2,8,8,8,128]{6,5,4,3,2,0,1:T(8,128)(2,1)S(1)}, u32[]{:S(2)}, u32[]{:S(2)}) collective-permute-start(bf16[2,1,2,8,8,8,128]{6,5,4,3,2,0,1:T(8,128)(2,1)S(1)} %get-tuple-element.122), channel_id=1, source_target_pairs={{2,0},{4,2},{6,4},{8,6},{10,8},{12,10},{14,12},{16,14},{18,16},{20... | collective-permute-start | bytes 1572872 | tf_op jit(solution)/shard_map/ppermute | solution.py:26
  21.7 23.4 %copy-start.129 = (pred[4]{0:T(512)(128)(4,1)}, pred[4]{0:T(512)(128)(4,1)S(1)}, u32[]{:S(2)}) copy-start(pred[4]{0:T(512)(128)(4,1)S(1)} %compare_and_fusion.27) | copy-start | bytes 16
  28.8 15.6 copy-start.104
  45.1 3.8 copy-start.40
  45.3 23.6 %collective-permute-start.2 = (bf16[2,4,8,8,8,128]{5,4,3,2,0,1:T(8,128)(2,1)S(1)}, bf16[2,4,8,8,8,128]{5,4,3,2,0,1:T(8,128)(2,1)S(1)}, u32[]{:S(2)}, u32[]{:S(2)}) collective-permute-start(bf16[2,4,8,8,8,128]{5,4,3,2,0,1:T(8,128)(2,1)S(1)} %select_bitcast_fusion), channel_id=1, source_target_pairs={{0,1},{1,0},{2,3},{3,2},{4,5},{5,4},{6,7},{7,6},{8,9},{9,8},{10,11... | collective-permute-start | bytes 3145736 | tf_op jit(solution)/shard_map/ppermute | solution.py:32
  152.8 11.6 copy-start.87
  152.8 11.6 copy-start.88
  157.4 14.5 copy-start.61
  157.4 14.5 copy-start.62
  158.9 14.5 copy-start.63
  159.0 14.4 copy-start.64
  180.2 4.9 copy-start.92
  180.2 5.6 copy-start.100
  180.2 6.4 copy-start.102
  180.3 7.1 copy-start.96
  180.3 8.6 copy-start.94
  180.3 10.3 copy-start.91
  197.5 3.6 copy-start.76
  197.5 4.3 copy-start.75
  279.7 8.8 copy-start.44
  279.9 9.5 collective-permute-start.3
  285.7 9.2 collective-permute-start.4
  296.8 10.3 collective-permute-start.5
  297.6 1376.5 %all-reduce.9.cloned.1.call-start = ((), (), s32[]{:S(2)}) async-start(), calls=%async_computation | async-start | bytes 7077888 | tf_op jit(solution)/shard_map/psum | solution.py:14
  309.8 6.1 copy-start.106
  309.8 7.1 copy-start.116
  309.8 7.9 copy-start.117
  310.5 8.0 copy-start.110
  311.2 8.1 copy-start.108
  311.3 8.3 copy-start.109
  312.8 10.7 copy-start.107
  313.5 13.6 copy-start.131
  314.1 9.5 copy-start.58
  314.1 10.9 copy-start.57
  314.1 12.3 copy-start.56
  314.1 13.0 copy-start.55
  314.1 13.7 copy-start.115
  315.9 13.4 copy-start.95
  316.0 15.5 copy-start.93
  316.0 16.1 copy-start.74
  316.0 16.8 copy-start.101
  316.1 17.4 %copy-start.73 = (bf16[11,1,1,1,128]{4,3,2,1,0:T(2,128)(2,1)S(1)}, bf16[11,1,1,1,128]{4,3,2,1,0:T(2,128)(2,1)}, u32[]{:S(2)}) copy-start(bf16[11,1,1,1,128]{4,3,2,1,0:T(2,128)(2,1)} %get-tuple-element.46) | copy-start | bytes 8452
  316.1 18.1 %copy-start.103 = (pred[2]{0:T(512)(128)(4,1)S(1)}, pred[2]{0:T(512)(128)(4,1)}, u32[]{:S(2)}) copy-start(pred[2]{0:T(512)(128)(4,1)} %get-tuple-element.272) | copy-start | bytes 10
  316.1 18.8 %copy-start.72 = (bf16[11,1,1,1,128]{4,3,2,1,0:T(2,128)(2,1)S(1)}, bf16[11,1,1,1,128]{4,3,2,1,0:T(2,128)(2,1)}, u32[]{:S(2)}) copy-start(bf16[11,1,1,1,128]{4,3,2,1,0:T(2,128)(2,1)} %get-tuple-element.47) | copy-start | bytes 8452
  316.1 20.0 %copy-start.71 = (bf16[11,1,1,1,128]{4,3,2,1,0:T(2,128)(2,1)S(1)}, bf16[11,1,1,1,128]{4,3,2,1,0:T(2,128)(2,1)}, u32[]{:S(2)}) copy-start(bf16[11,1,1,1,128]{4,3,2,1,0:T(2,128)(2,1)} %get-tuple-element.44) | copy-start | bytes 8452
  337.7 3.4 copy-start.105
  337.7 3.5 copy-start.54
  337.7 4.2 copy-start.114
  337.7 4.3 copy-start.53
  337.7 5.0 copy-start.112
  337.7 6.5 copy-start.113
  337.7 8.0 copy-start.111
  337.7 8.0 copy-start.70
  337.7 8.7 copy-start.121
  337.8 8.8 copy-start.69
  337.8 9.5 copy-start.120
  337.8 9.6 copy-start.68
  337.8 10.2 copy-start.118
  337.8 10.3 copy-start.67
  337.8 11.0 copy-start.119
  (79 other events, 119.9 us)
Sparse Core Ops, SparseCore 0:
  297.8 111.1 all-reduce.10
  411.7 1262.4 all-reduce.8
